TPU v7x, 32 devices: a whole 2x2x4 slice. The times are simulated.
32 devices in a mesh: req: 8 (over z, x), head: 4 (over y, core).
Axes of the slice: x: 2, y: 2, z: 4, core: 2. Of those that a mesh axis runs over, the one named last changes fastest.
Arguments:
- hidden_state: bfloat16 [64, 2048], P('req'), may hold values from -6 to 6
- attend_gain: float32 [2048], replicated, may hold values from 0.1 to 1.9
- input_weight: bfloat16 [2048, 3, 2048], P(None, None, 'head'), may hold values from -0.125 to 0.125
- input_bias: float32 [3, 2048], P(None, 'head'), may hold values from -3 to 3
- output_weight: bfloat16 [2048, 2048], P('head'), may hold values from -0.125 to 0.125
- window_cache: bfloat16 [64, 2, 2048, 2048], P('req', None, None, 'head'), may hold values from -9 to 9
- sink_cache: bfloat16 [64, 2, 4, 2048], P('req', None, None, 'head'), may hold values from -3000 to 3000
- lengths: int32 [64], P('req'), may hold values from 16 to 32768, as said below
- expert_index: int32 [64, 4], P('req'), may hold values from 0 to 31, all different within a row; in each aligned block of 8 rows (0 to 7, 8 to 15, ...) at most 2 rows name the same one
- router_weight: float32 [64, 4], P('req'), may hold values from 0.05 to 0.5
- mixture_gain: float32 [2048], replicated, may hold values from 0.1 to 1.9
- expert_gate_up: bfloat16 [2, 45056, 2048], P(None, ('req', 'head')), may hold values from -0.125 to 0.125
- expert_down: bfloat16 [45056, 2048], P(('req', 'head')), may hold values from -0.3125 to 0.3125
- shared_gate_up: bfloat16 [2, 2048, 5632], P(None, 'req', 'head'), may hold values from -0.125 to 0.125
- shared_down: bfloat16 [5632, 2048], P('head', 'req'), may hold values from -0.078125 to 0.078125
- shared_gate: float32 [2048], replicated, may hold values from -0.125 to 0.125
Outputs:
- layer_out: bfloat16 [64, 2048], P('req', 'head')
- new_kv: bfloat16 [64, 2, 2048], P('req', None, 'head')
Inputs may be any that keep to these rules, and one draw needn't show every extreme that they name: Request r has lengths[r] cached tokens and its new token takes position lengths[r]; some request has exactly 32768 cached tokens and some has 16. `expert_index`: each row names 4 different experts; within the rows of one index of req (aligned blocks of 8 rows) no expert is named more than 2 times, a bound that some block reaches.
All inputs are finite; a program needn't handle non-finite values.
Results may differ from a plain program's by a relative error of at most 0.014.
The roundings to bfloat16 on the way count: a program that leaves them out, or rounds other values in their place, can miss the bound.
Values may be sent and summed in bfloat16 or wider, within the bound.
No kernel may reach another device: no remote copies, remote signals or barrier semaphores. Data moves between devices by JAX's collectives and lax.ppermute only.
A program may use at most 256 MiB of HBM per device.

v0:
```python
import math
import jax
import jax.numpy as jnp
from jax import lax
from jax.sharding import PartitionSpec as P

HD = 128
EXPERTS = 32
FE = 1408
SINKS = 4
CAP = 2
EPSILON = 1e-06
ROPE_BASE = 1000000.0


def rms_scale(values, gains):
    mean_square = jnp.mean(values * values, axis=-1, keepdims=True)
    return values * lax.rsqrt(mean_square + EPSILON) * gains


def rotate(vectors, positions):
    half_depth = vectors.shape[-1] // 2
    steps_half = jnp.arange(half_depth).astype(jnp.float32)
    frequencies = jnp.float32(ROPE_BASE) ** (-(2.0 / vectors.shape[-1]) * steps_half)
    angles = positions.astype(jnp.float32)[:, None] * frequencies[None, :]
    cosine = jnp.cos(angles)[:, None, :]
    sine_terms = jnp.sin(angles)[:, None, :]
    lower_half = vectors[..., :half_depth]
    upper_half = vectors[..., half_depth:]
    return jnp.concatenate(
        [
            lower_half * cosine - upper_half * sine_terms,
            upper_half * cosine + lower_half * sine_terms,
        ],
        axis=-1,
    )


def block_scores(queries, fresh_key, window_cache, fresh_slot, live_count, block_size):
    row_count, head_count, head_depth = queries.shape
    key_rows = window_cache[:, 0].reshape(row_count, block_size, head_count, head_depth)
    scores = jnp.einsum("rhd,rshd->rhs", queries, key_rows, preferred_element_type=jnp.float32)
    fresh_scores = jnp.einsum("rhd,rhd->rh", queries, fresh_key, preferred_element_type=jnp.float32)
    positions = jnp.arange(block_size)
    is_fresh = positions[None, :] == fresh_slot[:, None]
    scores = jnp.where(is_fresh[:, None, :], fresh_scores[:, :, None], scores) / math.sqrt(
        head_depth
    )
    keeping = positions[None, :] < live_count[:, None]
    return jnp.where(keeping[:, None, :], scores, -jnp.inf)


def block_values(window_cache, block_size, head_count, head_depth):
    row_count = window_cache.shape[0]
    return window_cache[:, 1].reshape(row_count, block_size, head_count, head_depth)


def window_values(weights, is_fresh, value_rows, fresh_value):
    kept_weights = jnp.where(is_fresh[:, None, :], jnp.zeros_like(weights), weights)
    fresh_weight = jnp.sum(
        jnp.where(is_fresh[:, None, :], weights, jnp.zeros_like(weights)), axis=-1
    )
    window_part = jnp.einsum(
        "rhs,rshd->rhd", kept_weights, value_rows, preferred_element_type=jnp.float32
    )
    return window_part + fresh_weight.astype(jnp.float32)[..., None] * fresh_value.astype(
        jnp.float32
    )


def expert_slice(arrived, expert_gate_up, expert_down):
    gate_terms = jnp.einsum(
        "nkd,fd->nkf", arrived, expert_gate_up[0], preferred_element_type=jnp.float32
    )
    up_terms = jnp.einsum(
        "nkd,fd->nkf", arrived, expert_gate_up[1], preferred_element_type=jnp.float32
    )
    hidden_units = (jax.nn.silu(gate_terms) * up_terms).astype(jnp.bfloat16)
    return jnp.einsum("nkf,fd->nkd", hidden_units, expert_down, preferred_element_type=jnp.float32)


def local(
    hidden_state,
    attend_gain,
    input_weight,
    input_bias,
    output_weight,
    window_cache,
    sink_cache,
    lengths,
    expert_index,
    router_weight,
    mixture_gain,
    expert_gate_up,
    expert_down,
    shared_gate_up,
    shared_down,
    shared_gate,
):
    row_count, model_width = hidden_state.shape
    local_width = input_weight.shape[2]
    head_depth = HD
    head_count = local_width // head_depth
    window_length = window_cache.shape[2]
    normed = rms_scale(hidden_state.astype(jnp.float32), attend_gain).astype(jnp.bfloat16)
    projected = jnp.dot(
        normed,
        input_weight.reshape(model_width, 3 * local_width),
        preferred_element_type=jnp.float32,
    ) + input_bias.reshape(3 * local_width)
    projected = projected.reshape(row_count, 3, head_count, head_depth)
    queries = rotate(projected[:, 0], lengths).astype(jnp.bfloat16)
    fresh_key = rotate(projected[:, 1], lengths).astype(jnp.bfloat16)
    fresh_value = projected[:, 2].astype(jnp.bfloat16)
    new_kv = jnp.stack(
        [fresh_key.reshape(row_count, local_width), fresh_value.reshape(row_count, local_width)],
        axis=1,
    )
    fresh_slot = (lengths - SINKS) % window_length
    live_count = jnp.minimum(lengths - SINKS + 1, window_length)
    sink_keys = sink_cache[:, 0].reshape(row_count, SINKS, head_count, head_depth)
    sink_values = sink_cache[:, 1].reshape(row_count, SINKS, head_count, head_depth)
    sink_scores = jnp.einsum(
        "rhd,rshd->rhs", queries, sink_keys, preferred_element_type=jnp.float32
    ) / math.sqrt(head_depth)
    scores = block_scores(queries, fresh_key, window_cache, fresh_slot, live_count, window_length)
    is_fresh = jnp.arange(window_length)[None, :] == fresh_slot[:, None]
    value_rows = block_values(window_cache, window_length, head_count, head_depth)
    score_peak = jnp.maximum(jnp.max(sink_scores, axis=-1), jnp.max(scores, axis=-1))
    window_exp = jnp.exp(scores - score_peak[..., None])
    score_total = jnp.sum(jnp.exp(sink_scores - score_peak[..., None]), axis=-1) + jnp.sum(
        window_exp, axis=-1
    )
    weights = (window_exp / score_total[..., None]).astype(jnp.bfloat16)
    accum = window_values(weights, is_fresh, value_rows, fresh_value)
    sink_weights = (jnp.exp(sink_scores - score_peak[..., None]) / score_total[..., None]).astype(
        jnp.bfloat16
    )
    accum = accum + jnp.einsum(
        "rhs,rshd->rhd", sink_weights, sink_values, preferred_element_type=jnp.float32
    )
    attended = accum.astype(jnp.bfloat16).reshape(row_count, local_width)
    attend_part = jnp.dot(attended, output_weight, preferred_element_type=jnp.float32)
    resid = hidden_state.astype(jnp.float32) + lax.psum(attend_part, "head")
    tokens = rms_scale(resid, mixture_gain).astype(jnp.bfloat16)
    all_tokens = lax.all_gather(tokens, "req", axis=0, tiled=True)
    group_index = lax.axis_index("req")
    group_count = lax.axis_size("req")
    row_width = shared_gate_up.shape[1]
    my_columns = lax.dynamic_slice_in_dim(all_tokens, group_index * row_width, row_width, 1)
    shared_terms = jnp.einsum(
        "td,cdf->ctf", my_columns, shared_gate_up, preferred_element_type=jnp.float32
    )
    shared_terms = lax.psum(shared_terms, "req")
    shared_hidden = (jax.nn.silu(shared_terms[0]) * shared_terms[1]).astype(jnp.bfloat16)
    gate_value = jax.nn.sigmoid(
        jnp.dot(all_tokens.astype(jnp.float32), shared_gate, precision=lax.Precision.HIGHEST)
    )
    shared_out = gate_value[:, None] * jnp.dot(
        shared_hidden, shared_down, preferred_element_type=jnp.float32
    )
    expert_hot = (expert_index[:, :, None] == jnp.arange(EXPERTS)[None, None, :]).astype(
        jnp.float32
    )
    combine = jnp.sum(expert_hot * router_weight[:, :, None], axis=1)
    local_experts = EXPERTS // group_count
    quarters = FE // expert_down.shape[0]
    local_pick = lax.axis_index("head") // quarters
    expert_hit = jnp.sum(expert_hot, axis=1)
    slot_rank = jnp.cumsum(expert_hit, axis=0) - expert_hit
    chosen = expert_hit[:, :, None] * (
        slot_rank[:, :, None] == jnp.arange(CAP)[None, None, :]
    ).astype(jnp.float32)
    mine_hot = (jnp.arange(local_experts) == local_pick).astype(jnp.float32)
    chosen_mine = jnp.einsum(
        "rglc,l->rgc",
        chosen.reshape(row_count, group_count, local_experts, CAP),
        mine_hot,
        precision=lax.Precision.HIGHEST,
    )
    combine_mine = jnp.einsum(
        "rgl,l->rg",
        combine.reshape(row_count, group_count, local_experts),
        mine_hot,
        precision=lax.Precision.HIGHEST,
    )
    placing = chosen_mine.reshape(row_count, group_count * CAP)
    outgoing = jnp.dot(
        placing.T.astype(jnp.bfloat16), tokens, preferred_element_type=jnp.float32
    ).astype(jnp.bfloat16)
    outgoing = outgoing.reshape(group_count, CAP, model_width)
    produced = expert_slice(
        lax.all_to_all(outgoing, "req", split_axis=0, concat_axis=0, tiled=True),
        expert_gate_up,
        expert_down,
    )
    returned = lax.all_to_all(produced, "req", split_axis=0, concat_axis=0, tiled=True)
    weighting = (chosen_mine * combine_mine[:, :, None]).reshape(row_count, group_count * CAP)
    routed = jnp.dot(
        weighting,
        returned.reshape(group_count * CAP, model_width),
        precision=lax.Precision.HIGHEST,
        preferred_element_type=jnp.float32,
    )
    routed = routed + lax.all_to_all(shared_out, "req", split_axis=0, concat_axis=1, tiled=True)
    final = lax.psum_scatter(routed, "head", scatter_dimension=1, tiled=True)
    slice_width = final.shape[1]
    own_resid = lax.dynamic_slice_in_dim(
        resid, lax.axis_index("head") * slice_width, slice_width, 1
    )
    return ((own_resid + final).astype(jnp.bfloat16), new_kv)


def solution(mesh):
    return jax.shard_map(
        local,
        mesh=mesh,
        in_specs=(
            P("req", None),
            P(),
            P(None, None, "head"),
            P(None, "head"),
            P("head", None),
            P("req", None, None, "head"),
            P("req", None, None, "head"),
            P("req"),
            P("req", None),
            P("req", None),
            P(),
            P(None, ("req", "head"), None),
            P(("req", "head"), None),
            P(None, "req", "head"),
            P("head", "req"),
            P(),
        ),
        out_specs=(P("req", "head"), P("req", None, "head")),
        check_vma=False,
    )
```

profile of v0, /device:TPU:0, one launch (start us, length us, event | category | flops | bytes accessed | tf_op | source)
XLA Modules:
  0.0 306.4 jit_solution(18246826656507924227)
XLA Ops:
  7.2 0.0 all-reduce.3.cloned.1.call-start
  7.3 0.8 and_select_fusion
  8.1 8.8 %copy.43 = bf16[2048,3,512]{0,2,1:T(8,128)(2,1)} copy(bf16[2048,3,512]{2,0,1:T(8,128)(2,1)} %param.18) | data formatting | bytes 12582912 | tf_op args[2]
  16.9 0.1 fusion.39
  17.1 4.5 %convolution_add_fusion = f32[8,1536]{1,0:T(8,128)S(1)} fusion(bf16[2048,1536]{0,1:T(8,128)(2,1)} %bitcast.145, bf16[8,2048]{1,0:T(8,128)(2,1)S(1)} %copy-done.4, f32[2048]{0:T(1024)S(1)} %copy-done.7, f32[8]{0:T(128)S(1)} %add_rsqrt_fusion.1, f32[1536]{0:T(1024)S(1)} %add.96), kind=kOutput, calls=%fused_computation.14 | convolution fusion | flops 50409472 | bytes 6387744 | tf_op jit(solution)/shard_map/dot_general | solution.py:106
  21.6 0.6 copy-done.5
  22.2 0.1 multiply_cosine_fusion
  22.3 0.1 subtract_convert_fusion
  22.4 0.1 multiply_subtract_fusion
  22.5 22.5 %fusion.80 = (bf16[8,1,2048,512]{3,2,1,0:T(8,128)(2,1)}, bf16[8,1,2048,512]{3,2,1,0:T(8,128)(2,1)}) fusion(bf16[8,2,2048,512]{3,2,1,0:T(8,128)(2,1)} %param.21), kind=kLoop, calls=%fused_computation.124 | loop fusion | bytes 67108864 | tf_op jit(solution)/shard_map/slice | solution.py:55
  45.0 21.6 %copy.77 = bf16[8,1,2048,512]{2,3,0,1:T(8,128)(2,1)} copy(bf16[8,1,2048,512]{3,2,1,0:T(8,128)(2,1)} %get-tuple-element.17) | data formatting | bytes 33554432 | tf_op jit(solution)/shard_map/reshape;squeeze | solution.py:41
  66.6 0.1 fusion.72
  66.7 8.0 %fusion.58 = f32[8,4,1,2048]{3,2,1,0:T(1,128)S(1)} fusion(bf16[8,2048,4,128]{1,3,2,0:T(8,128)(2,1)} %bitcast.144, bf16[8,4,128,1]{2,0,1,3:T(8,128)(2,1)S(1)} %fusion.72), kind=kOutput, calls=%fused_computation.87 | convolution fusion | flops 16777216 | bytes 17047552 | tf_op jit(solution)/shard_map/rhd,rshd->rhs/dot_general | solution.py:42
  74.8 0.2 fusion.51
  74.9 0.1 copy.62
  75.0 0.7 fusion.56
  75.7 0.1 iota_compare_fusion
  75.8 0.3 fusion.32
  76.1 0.3 fusion.29
  76.5 0.3 select_reduce_fusion
  76.8 0.7 select_bitcast_fusion
  77.5 23.7 %reshape_squeeze.14 = bf16[8,2048,4,128]{3,2,1,0:T(4,128)(2,1)} reshape(bf16[8,1,2048,512]{3,2,1,0:T(8,128)(2,1)} %get-tuple-element.16) | data formatting | bytes 33554432 | tf_op jit(solution)/shard_map/reshape;squeeze | solution.py:55
  101.1 0.1 copy.66
  101.3 0.1 fusion.52
  101.4 8.3 %fusion = f32[8,4,1,128]{3,2,1,0:T(1,128)S(1)} fusion(bf16[8,2048,4,128]{3,2,1,0:T(4,128)(2,1)} %reshape_squeeze.14, bf16[8,4,2048,1]{2,0,1,3:T(8,128)(2,1)} %select_bitcast_fusion), kind=kOutput, calls=%fused_computation | convolution fusion | flops 16777216 | bytes 16924672 | tf_op jit(solution)/shard_map/rhs,rshd->rhd/dot_general | solution.py:63
  109.8 1.8 fusion.61
  111.5 0.0 all-reduce.3.cloned.1.call-update
  111.6 0.5 iota_convert_fusion
  112.1 0.7 select_reduce_fusion.1
  112.8 0.8 copy.44
  113.5 0.7 copy.46
  114.3 3.2 %reduce_window_sum.14 = f32[8,8,4]{0,2,1:T(4,128)} reduce-window(f32[8,8,4]{0,2,1:T(4,128)S(1)} %bitcast.147, f32[]{:T(128)} %constant.67.clone.1), window={size=8x1x1 pad=7_0x0_0x0_0}, to_apply=%region_8.9 | reduce-window | flops 1792 | bytes 2052 | tf_op jit(solution)/shard_map/jit(cumsum)/reduce_window_sum | solution.py:170
  117.4 1.3 sub.46
  118.8 1.4 copy.45
  120.2 1.6 multiply_reduce_fusion
  121.8 1.5 copy.74
  123.3 0.7 copy.47
  124.0 0.1 fusion.70
  124.2 0.8 broadcast_multiply_fusion
  124.9 20.5 %all-reduce.3.cloned.1.call-done = f32[8,2048]{1,0:T(8,128)} async-done(((f32[8,2048]{1,0:T(8,128)}), f32[8,2048]{1,0:T(8,128)}) %all-reduce.3.cloned.1.call-update) | async-done | bytes 65552 | tf_op jit(solution)/shard_map/psum | solution.py:144
  145.5 1.0 multiply_reduce_fusion.1
  146.4 0.6 copy-done.3
  147.0 0.8 multiply_convert_fusion
  147.8 32.8 %all_gather.3 = bf16[64,2048]{1,0:T(8,128)(2,1)} all-gather(bf16[8,2048]{1,0:T(8,128)(2,1)S(1)} %multiply_convert_fusion), channel_id=1, replica_groups=mesh['req'=8,'head'=4] {'req'}, dimensions={0}, use_global_device_ids=true | all-gather | bytes 294912 | tf_op jit(solution)/shard_map/all_gather | solution.py:146
  180.6 0.8 convolution_convert_fusion
  181.4 1.5 reshape.198
  182.9 5.4 %all-to-all-start = ((bf16[8,2,2048]{2,1,0:T(2,128)(2,1)}), bf16[8,2,2048]{2,1,0:T(2,128)(2,1)}, u32[]{:S(2)}, u32[]{:S(2)}) async-start(bf16[8,2,2048]{2,1,0:T(2,128)(2,1)} %reshape.198), calls=%async_computation | async-start | bytes 131072 | tf_op jit(solution)/shard_map/all_to_all | solution.py:193
  188.3 0.2 all-reduce.5.cloned.1.call-start
  188.6 2.0 convolution_bitcast_fusion
  190.6 4.7 %all-to-all-done = bf16[8,2,2048]{2,1,0:T(2,128)(2,1)} async-done(((bf16[8,2,2048]{2,1,0:T(2,128)(2,1)}), bf16[8,2,2048]{2,1,0:T(2,128)(2,1)}, u32[]{:S(2)}, u32[]{:S(2)}) %all-to-all-start) | async-done | bytes 65568 | tf_op jit(solution)/shard_map/all_to_all | solution.py:193
  195.3 4.3 %fusion.6 = f32[8,2,1408]{2,0,1:T(8,128)S(1)} fusion(bf16[2,1408,2048]{2,1,0:T(8,128)(2,1)} %param.27, bf16[8,2,2048]{2,1,0:T(2,128)(2,1)} %all-to-all-done), kind=kOutput, calls=%fused_computation.6 | convolution fusion | flops 92274688 | bytes 5922816 | tf_op jit(solution)/shard_map/nkd,fd->nkf/dot_general | solution.py:72
  199.6 7.1 %fusion.2 = f32[8,2,2048]{2,0,1:T(8,128)S(1)} fusion(bf16[1408,2048]{1,0:T(8,128)(2,1)} %param.28, bf16[2,1408,2048]{2,1,0:T(8,128)(2,1)} %param.27, f32[8,2,1408]{2,0,1:T(8,128)S(1)} %fusion.6, bf16[8,2,2048]{2,1,0:T(2,128)(2,1)} %all-to-all-done), kind=kOutput, calls=%fused_computation.2 | convolution fusion | flops 184684544 | bytes 11821056 | tf_op jit(solution)/shard_map/nkf,fd->nkd/dot_general | solution.py:79
  206.6 0.8 copy.50
  207.4 3.4 %all-to-all-start.1 = ((f32[8,2,2048]{2,1,0:T(2,128)}), f32[8,2,2048]{2,1,0:T(2,128)S(1)}, u32[]{:S(2)}, u32[]{:S(2)}) async-start(f32[8,2,2048]{2,1,0:T(2,128)} %copy.50), calls=%async_computation.1 | async-start | bytes 262144 | tf_op jit(solution)/shard_map/all_to_all | solution.py:197
  210.8 0.0 reduce-scatter.2.cloned.1.call-start
  210.9 0.3 fusion.21
  211.2 57.6 %all-reduce.5.cloned.1.call-done = f32[2,64,1408]{2,1,0:T(8,128)} async-done(((f32[2,64,1408]{2,1,0:T(8,128)}), f32[2,64,1408]{2,1,0:T(8,128)}) %all-reduce.5.cloned.1.call-update) | async-done | bytes 720912 | tf_op jit(solution)/shard_map/psum | solution.py:154
  268.7 1.4 fusion.17
  270.1 10.4 %all_to_all.29 = f32[8,8,256]{2,1,0:T(8,128)S(1)} all-to-all(f32[8,8,256]{2,1,0:T(8,128)S(1)} %fusion.17), channel_id=1, replica_groups=mesh['req'=8,'head'=4] {'req'}, dimensions={0} | all-to-all | bytes 131072 | tf_op jit(solution)/shard_map/all_to_all | solution.py:205
  280.5 0.9 fusion.16
  281.4 0.7 fusion.69
  282.2 0.6 copy.53
  282.8 15.7 %reduce-scatter.2.cloned.1.call-done = f32[8,512]{1,0:T(8,128)} async-done(((f32[8,2048]{1,0:T(8,128)}), f32[8,512]{1,0:T(8,128)}) %reduce-scatter.2.cloned.1.call-update) | async-done | bytes 16400 | tf_op jit(solution)/shard_map/reduce_scatter | solution.py:206
  298.5 1.3 add_convert_fusion
  (42 shorter events, 0.2 us)
Async XLA Ops:
  7.2 102.6 %copy-start = (bf16[512,2048]{1,0:T(8,128)(2,1)S(1)}, bf16[512,2048]{1,0:T(8,128)(2,1)}, u32[]{:S(2)}) copy-start(bf16[512,2048]{1,0:T(8,128)(2,1)} %param.20) | copy-start | bytes 6291460
  7.2 9.7 %copy-start.8 = (f32[3,512]{1,0:T(4,128)S(1)}, f32[3,512]{1,0:T(4,128)}, u32[]{:S(2)}) copy-start(f32[3,512]{1,0:T(4,128)} %param.19) | copy-start | bytes 18436
  7.2 9.7 %copy-start.4 = (bf16[8,2048]{1,0:T(8,128)(2,1)S(1)}, bf16[8,2048]{1,0:T(8,128)(2,1)}, u32[]{:S(2)}) copy-start(bf16[8,2048]{1,0:T(8,128)(2,1)} %param.16) | copy-start | bytes 98308
  7.2 9.9 %copy-start.7 = (f32[2048]{0:T(1024)S(1)}, f32[2048]{0:T(1024)}, u32[]{:S(2)}) copy-start(f32[2048]{0:T(1024)} %param.17) | copy-start | bytes 24580
  7.2 138.2 %all-reduce.3.cloned.1.call-start = ((), (), s32[]{:S(2)}) async-start(), calls=%async_computation.4 | async-start | bytes 131072 | tf_op jit(solution)/shard_map/psum | solution.py:144
  21.6 0.6 copy-start.5
  66.6 8.1 %copy-start.12 = (bf16[8,2,4,512]{3,2,1,0:T(4,128)(2,1)S(1)}, bf16[8,2,4,512]{3,2,1,0:T(4,128)(2,1)}, u32[]{:S(2)}) copy-start(bf16[8,2,4,512]{3,2,1,0:T(4,128)(2,1)} %param.22) | copy-start | bytes 196612
  101.4 10.7 %copy-start.9 = (f32[8,4]{0,1:T(4,128)S(1)}, f32[8,4]{0,1:T(4,128)}, u32[]{:S(2)}) copy-start(f32[8,4]{0,1:T(4,128)} %param.25) | copy-start | bytes 388
  101.4 10.7 %copy-start.10 = (s32[8,4]{0,1:T(4,128)S(1)}, s32[8,4]{0,1:T(4,128)}, u32[]{:S(2)}) copy-start(s32[8,4]{0,1:T(4,128)} %param.24) | copy-start | bytes 388
  101.4 87.1 %copy-start.1 = (bf16[2,256,1408]{2,1,0:T(8,128)(2,1)S(1)}, bf16[2,256,1408]{2,1,0:T(8,128)(2,1)}, u32[]{:S(2)}) copy-start(bf16[2,256,1408]{2,1,0:T(8,128)(2,1)} %param.29) | copy-start | bytes 4325380
  146.4 0.6 copy-start.3
  182.9 12.4 %all-to-all-start = ((bf16[8,2,2048]{2,1,0:T(2,128)(2,1)}), bf16[8,2,2048]{2,1,0:T(2,128)(2,1)}, u32[]{:S(2)}, u32[]{:S(2)}) async-start(bf16[8,2,2048]{2,1,0:T(2,128)(2,1)} %reshape.198), calls=%async_computation | async-start | bytes 131072 | tf_op jit(solution)/shard_map/all_to_all | solution.py:193
  188.3 80.4 %all-reduce.5.cloned.1.call-start = ((), (), s32[]{:S(2)}) async-start(), calls=%async_computation.5 | async-start | bytes 1441792 | tf_op jit(solution)/shard_map/psum | solution.py:154
  190.6 20.3 %copy-start.2 = (bf16[64,2048]{1,0:T(8,128)(2,1)S(1)}, bf16[64,2048]{1,0:T(8,128)(2,1)}, u32[]{:S(2)}) copy-start(bf16[64,2048]{1,0:T(8,128)(2,1)} %all_gather.3) | copy-start | bytes 786436
  190.6 20.3 %copy-start.13 = (f32[2048]{0:T(1024)S(1)}, f32[2048]{0:T(1024)}, u32[]{:S(2)}) copy-start(f32[2048]{0:T(1024)} %param.31) | copy-start | bytes 24580
  190.6 78.1 %copy-start.11 = (bf16[1408,256]{1,0:T(8,128)(2,1)S(1)}, bf16[1408,256]{1,0:T(8,128)(2,1)}, u32[]{:S(2)}) copy-start(bf16[1408,256]{1,0:T(8,128)(2,1)} %param.30) | copy-start | bytes 2162692
  190.6 91.5 %copy-start.6 = (bf16[8,4,128]{2,0,1:T(8,128)(2,1)S(1)}, bf16[8,4,128]{2,0,1:T(8,128)(2,1)}, u32[]{:S(2)}) copy-start(bf16[8,4,128]{2,0,1:T(8,128)(2,1)} %get-tuple-element.15) | copy-start | bytes 24580
  207.4 62.7 %all-to-all-start.1 = ((f32[8,2,2048]{2,1,0:T(2,128)}), f32[8,2,2048]{2,1,0:T(2,128)S(1)}, u32[]{:S(2)}, u32[]{:S(2)}) async-start(f32[8,2,2048]{2,1,0:T(2,128)} %copy.50), calls=%async_computation.1 | async-start | bytes 262144 | tf_op jit(solution)/shard_map/all_to_all | solution.py:197
  210.8 87.7 %reduce-scatter.2.cloned.1.call-start = ((), (), s32[]{:S(2)}) async-start(), calls=%async_computation.6 | async-start | bytes 81920 | tf_op jit(solution)/shard_map/reduce_scatter | solution.py:206
Sparse Core Ops, SparseCore 0:
  111.7 33.7 all-reduce.2
  193.1 75.6 all-reduce.4
  281.6 16.9 reduce-scatter.1
where the time goes:
time: 309 us; the launch traced here: 306 us
  waiting for transfers between devices  98.6 us (32%)
  local copies, waits for them, and re-layouts  86.9 us (28%)
  blocking collectives  43.2 us (14%)
  matrix products  39.7 us (13%)
  other arithmetic  14.9 us (5%)
  between operations  14 us (5%)
  starting transfers between devices  9.11 us (3%)
    psum x1, waiting for transfers between devices, local(): shared_terms = lax.psum(shared_terms, 'req')  57.6 us
    all_gather x1, blocking collectives, local(): all_tokens = lax.all_gather(tokens, 'req', axis=0, tiled=True)  32.8 us
    another operation x1, local copies, waits for them, and re-layouts, block_values(): window_cache[:, 1].reshape(row_count, block_size, head_count, head_depth)  23.7 us
    slice x1, local copies, waits for them, and re-layouts, block_values(): window_cache[:, 1].reshape(row_count, block_size, head_count, head_depth)  22.5 us
    another operation x1, local copies, waits for them, and re-layouts, block_scores(): window_cache[:, 0].reshape(row_count, block_size, head_count, head_depth)  21.6 us
    psum x1, waiting for transfers between devices, local(): resid = hidden_state.astype(jnp.float32) + lax.psum(attend_part, 'head')  20.5 us
    reduce_scatter x1, waiting for transfers between devices, local(): final = lax.psum_scatter(routed, 'head', scatter_dimension=1, tiled=True)  15.7 us
    unnamed x30, local copies, waits for them, and re-layouts  10.8 us
  transfers between devices with their start and end apart: 5, of which 4 were waited for; matrix products, arithmetic and copies ran while one was open for 10% of the time, Pallas kernels for 0%

commit v1 on v0

--- a/solution.py
+++ b/solution.py
@@ -143,7 +143,14 @@
     attend_part = jnp.dot(attended, output_weight, preferred_element_type=jnp.float32)
     resid = hidden_state.astype(jnp.float32) + lax.psum(attend_part, "head")
     tokens = rms_scale(resid, mixture_gain).astype(jnp.bfloat16)
-    all_tokens = lax.all_gather(tokens, "req", axis=0, tiled=True)
+    size = lax.axis_size("req")
+    route = [(i, (i + 1) % size) for i in range(size)]
+    shards = [tokens]
+    for stride in range(1, size):
+        shards = [lax.ppermute(shards[0], "req", route), *shards]
+    whole = jnp.concatenate(shards, axis=0)
+    shift = (lax.axis_index("req") + 1) * shards[-1].shape[0]
+    all_tokens = jnp.roll(whole, shift, axis=0)
     group_index = lax.axis_index("req")
     group_count = lax.axis_size("req")
     row_width = shared_gate_up.shape[1]

time: 309 us -> 331 us (1.071)
  blocking collectives: 43.2 us -> 10.4 us
  waiting for transfers between devices: 98.6 us -> 130 us
  local copies, waits for them, and re-layouts: 86.9 us -> 99 us
  starting transfers between devices: 9.11 us -> 13.5 us
    all_gather x1 -> x0, blocking collectives: 32.8 us -> none  [local(): all_tokens = lax.all_gather(tokens, 'req', axis=0, tiled=True)]
    ppermute x0 -> x7, waiting for transfers between devices: none -> 29.4 us  [local(): shards = [lax.ppermute(shards[0], 'req', route), *shards]]
    unnamed x30 -> x50, local copies, waits for them, and re-layouts: 10.8 us -> 22.8 us
    all_to_all x1, waiting for transfers between devices: 4.71 us -> 0.01 us  [local(): lax.all_to_all(outgoing, 'req', split_axis=0, concat_axis=0, tiled=True)]
    psum x1, waiting for transfers between devices: 57.6 us -> 62.1 us  [local(): shared_terms = lax.psum(shared_terms, 'req')]
    ppermute x0 -> x7, starting transfers between devices: none -> 3.51 us  [local(): shards = [lax.ppermute(shards[0], 'req', route), *shards]]
  transfers between devices with their start and end apart: 5 -> 12, of which waited for: 4 -> 9; matrix products, arithmetic and copies ran while one was open for 10% -> 10% of each run, Pallas kernels for 0% -> 0%
where the time goes in v1:
time: 331 us; the launch traced here: 327 us
  waiting for transfers between devices  130 us (39%)
  local copies, waits for them, and re-layouts  99 us (30%)
  matrix products  42.3 us (13%)
  other arithmetic  17.9 us (5%)
  between operations  14 us (4%)
  starting transfers between devices  13.5 us (4%)
  blocking collectives  10.4 us (3%)
    psum x1, waiting for transfers between devices, local(): shared_terms = lax.psum(shared_terms, 'req')  62.1 us
    ppermute x7, waiting for transfers between devices, local(): shards = [lax.ppermute(shards[0], 'req', route), *shards]  29.4 us
    another operation x1, local copies, waits for them, and re-layouts, block_values(): window_cache[:, 1].reshape(row_count, block_size, head_count, head_depth)  23.7 us
    psum x1, waiting for transfers between devices, local(): resid = hidden_state.astype(jnp.float32) + lax.psum(attend_part, 'head')  23.3 us
    unnamed x50, local copies, waits for them, and re-layouts  22.8 us
    slice x1, local copies, waits for them, and re-layouts, block_values(): window_cache[:, 1].reshape(row_count, block_size, head_count, head_depth)  22.5 us
    another operation x1, local copies, waits for them, and re-layouts, block_scores(): window_cache[:, 0].reshape(row_count, block_size, head_count, head_depth)  21.6 us
    reduce_scatter x1, waiting for transfers between devices, local(): final = lax.psum_scatter(routed, 'head', scatter_dimension=1, tiled=True)  15.1 us
  transfers between devices with their start and end apart: 12, of which 9 were waited for; matrix products, arithmetic and copies ran while one was open for 10% of the time, Pallas kernels for 0%

profile of v1, /device:TPU:0, one launch (start us, length us, event | category | flops | bytes accessed | tf_op | source)
XLA Modules:
  0.0 327.1 jit_solution(13745163893459190367)
XLA Ops:
  7.3 0.8 and_select_fusion
  8.1 8.9 %copy.43 = bf16[2048,3,512]{0,2,1:T(8,128)(2,1)} copy(bf16[2048,3,512]{2,0,1:T(8,128)(2,1)} %param.18) | data formatting | bytes 12582912 | tf_op args[2]
  17.1 4.5 %convolution_add_fusion = f32[8,1536]{1,0:T(8,128)S(1)} fusion(bf16[2048,1536]{0,1:T(8,128)(2,1)} %bitcast.144, bf16[8,2048]{1,0:T(8,128)(2,1)S(1)} %copy-done.3, f32[2048]{0:T(1024)S(1)} %copy-done.9, f32[8]{0:T(128)S(1)} %add_rsqrt_fusion.1, f32[1536]{0:T(1024)S(1)} %add.111), kind=kOutput, calls=%fused_computation.14 | convolution fusion | flops 50409472 | bytes 6387744 | tf_op jit(solution)/shard_map/dot_general | solution.py:106
  22.5 22.5 %fusion.81 = (bf16[8,1,2048,512]{3,2,1,0:T(8,128)(2,1)}, bf16[8,1,2048,512]{3,2,1,0:T(8,128)(2,1)}) fusion(bf16[8,2,2048,512]{3,2,1,0:T(8,128)(2,1)} %param.21), kind=kLoop, calls=%fused_computation.141 | loop fusion | bytes 67108864 | tf_op jit(solution)/shard_map/slice | solution.py:55
  45.0 21.6 %copy.77 = bf16[8,1,2048,512]{2,3,0,1:T(8,128)(2,1)} copy(bf16[8,1,2048,512]{3,2,1,0:T(8,128)(2,1)} %get-tuple-element.17) | data formatting | bytes 33554432 | tf_op jit(solution)/shard_map/reshape;squeeze | solution.py:41
  66.7 8.0 %fusion.59 = f32[8,4,1,2048]{3,2,1,0:T(1,128)S(1)} fusion(bf16[8,2048,4,128]{1,3,2,0:T(8,128)(2,1)} %bitcast.143, bf16[8,4,128,1]{2,0,1,3:T(8,128)(2,1)S(1)} %fusion.73), kind=kOutput, calls=%fused_computation.104 | convolution fusion | flops 16777216 | bytes 17047552 | tf_op jit(solution)/shard_map/rhd,rshd->rhs/dot_general | solution.py:42
  75.0 0.7 fusion.57
  76.8 23.7 %reshape_squeeze.14 = bf16[8,2048,4,128]{3,2,1,0:T(4,128)(2,1)} reshape(bf16[8,1,2048,512]{3,2,1,0:T(8,128)(2,1)} %get-tuple-element.16) | data formatting | bytes 33554432 | tf_op jit(solution)/shard_map/reshape;squeeze | solution.py:55
  100.8 9.2 %fusion = f32[8,4,1,128]{3,2,1,0:T(1,128)S(1)} fusion(bf16[8,2048,4,128]{3,2,1,0:T(4,128)(2,1)} %reshape_squeeze.14, bf16[8,4,2048,1]{2,0,1,3:T(8,128)(2,1)S(1)} %select_bitcast_fusion), kind=kOutput, calls=%fused_computation | convolution fusion | flops 16777216 | bytes 16924672 | tf_op jit(solution)/shard_map/rhs,rshd->rhd/dot_general | solution.py:63
  110.1 1.9 fusion.62
  113.1 0.8 copy.47
  113.9 0.7 fusion.71
  115.2 0.7 copy.44
  116.0 0.7 copy.46
  116.7 3.2 reduce_window_sum.14
  119.9 1.3 sub.50
  121.2 1.5 copy.45
  122.7 23.3 %all-reduce.3.cloned.1.call-done = f32[8,2048]{1,0:T(8,128)} async-done(((f32[8,2048]{1,0:T(8,128)}), f32[8,2048]{1,0:T(8,128)}) %all-reduce.3.cloned.1.call-update) | async-done | bytes 65552 | tf_op jit(solution)/shard_map/psum | solution.py:144
  146.0 1.0 multiply_reduce_fusion.1
  147.6 1.4 multiply_convert_fusion
  148.9 1.5 collective-permute-start
  150.4 1.6 multiply_reduce_fusion
  152.0 1.5 copy.74
  153.5 2.4 collective-permute-done
  155.9 0.8 broadcast_multiply_fusion
  156.7 6.1 %collective-permute-done.1 = bf16[8,2048]{1,0:T(8,128)(2,1)} collective-permute-done((bf16[8,2048]{1,0:T(8,128)(2,1)}, bf16[8,2048]{1,0:T(8,128)(2,1)}, u32[]{:S(2)}, u32[]{:S(2)}) %collective-permute-start.1) | collective-permute-done | bytes 32800 | tf_op jit(solution)/shard_map/ppermute | solution.py:150
  162.8 1.5 convolution_convert_fusion
  164.3 1.5 reshape.198
  165.8 6.0 %all-to-all-start = ((bf16[8,2,2048]{2,1,0:T(2,128)(2,1)}), bf16[8,2,2048]{2,1,0:T(2,128)(2,1)}, u32[]{:S(2)}, u32[]{:S(2)}) async-start(bf16[8,2,2048]{2,1,0:T(2,128)(2,1)} %reshape.198), calls=%async_computation | async-start | bytes 131072 | tf_op jit(solution)/shard_map/all_to_all | solution.py:200
  171.9 2.0 collective-permute-start.3
  173.9 5.3 %collective-permute-done.3 = bf16[8,2048]{1,0:T(8,128)(2,1)S(1)} collective-permute-done((bf16[8,2048]{1,0:T(8,128)(2,1)}, bf16[8,2048]{1,0:T(8,128)(2,1)S(1)}, u32[]{:S(2)}, u32[]{:S(2)}) %collective-permute-start.3) | collective-permute-done | bytes 32800 | tf_op jit(solution)/shard_map/ppermute | solution.py:150
  179.8 6.7 %collective-permute-done.4 = bf16[8,2048]{1,0:T(8,128)(2,1)} collective-permute-done((bf16[8,2048]{1,0:T(8,128)(2,1)S(1)}, bf16[8,2048]{1,0:T(8,128)(2,1)}, u32[]{:S(2)}, u32[]{:S(2)}) %collective-permute-start.4) | collective-permute-done | bytes 32800 | tf_op jit(solution)/shard_map/ppermute | solution.py:150
  186.5 6.9 %collective-permute-done.5 = bf16[8,2048]{1,0:T(8,128)(2,1)} collective-permute-done((bf16[8,2048]{1,0:T(8,128)(2,1)}, bf16[8,2048]{1,0:T(8,128)(2,1)}, u32[]{:S(2)}, u32[]{:S(2)}) %collective-permute-start.5) | collective-permute-done | bytes 32800 | tf_op jit(solution)/shard_map/ppermute | solution.py:150
  193.4 4.9 %fusion.6 = f32[8,2,1408]{2,0,1:T(8,128)} fusion(bf16[2,1408,2048]{2,1,0:T(8,128)(2,1)} %param.27, bf16[8,2,2048]{2,1,0:T(2,128)(2,1)} %all-to-all-done), kind=kOutput, calls=%fused_computation.6 | convolution fusion | flops 92274688 | bytes 5922816 | tf_op jit(solution)/shard_map/nkd,fd->nkf/dot_general | solution.py:72
  198.4 2.0 collective-permute-done.6
  200.4 0.8 constant_dynamic-update-slice_fusion.15
  201.1 0.8 constant_dynamic-update-slice_fusion.14
  201.9 0.8 constant_dynamic-update-slice_fusion.13
  202.6 0.8 constant_dynamic-update-slice_fusion.12
  203.4 0.8 constant_dynamic-update-slice_fusion.11
  204.2 0.8 constant_dynamic-update-slice_fusion.10
  204.9 0.8 constant_dynamic-update-slice_fusion.9
  205.7 0.9 constant_dynamic-update-slice_fusion.8
  206.6 0.8 constant_dynamic-update-slice_fusion.7
  207.4 0.8 constant_dynamic-update-slice_fusion.6
  208.1 0.8 constant_dynamic-update-slice_fusion.5
  208.9 0.8 constant_dynamic-update-slice_fusion.4
  209.6 0.8 constant_dynamic-update-slice_fusion.3
  210.4 0.8 constant_dynamic-update-slice_fusion.2
  211.2 0.8 constant_dynamic-update-slice_fusion.1
  211.9 0.9 constant_dynamic-update-slice_fusion
  212.8 0.8 copy-done.5
  213.6 1.3 convolution_bitcast_fusion
  215.0 7.3 %fusion.2 = f32[8,2,2048]{2,0,1:T(8,128)S(1)} fusion(bf16[1408,2048]{1,0:T(8,128)(2,1)} %param.28, bf16[2,1408,2048]{2,1,0:T(8,128)(2,1)} %param.27, f32[8,2,1408]{2,0,1:T(8,128)} %fusion.6, bf16[8,2,2048]{2,1,0:T(2,128)(2,1)} %all-to-all-done), kind=kOutput, calls=%fused_computation.2 | convolution fusion | flops 184684544 | bytes 11821056 | tf_op jit(solution)/shard_map/nkf,fd->nkd/dot_general | solution.py:79
  222.3 0.8 copy.50
  223.0 3.9 %all-to-all-start.1 = ((f32[8,2,2048]{2,1,0:T(2,128)}), f32[8,2,2048]{2,1,0:T(2,128)S(1)}, u32[]{:S(2)}, u32[]{:S(2)}) async-start(f32[8,2,2048]{2,1,0:T(2,128)} %copy.50), calls=%async_computation.1 | async-start | bytes 262144 | tf_op jit(solution)/shard_map/all_to_all | solution.py:204
  227.3 62.1 %all-reduce.5.cloned.1.call-done = f32[2,64,1408]{2,1,0:T(8,128)} async-done(((f32[2,64,1408]{2,1,0:T(8,128)}), f32[2,64,1408]{2,1,0:T(8,128)}) %all-reduce.5.cloned.1.call-update) | async-done | bytes 720912 | tf_op jit(solution)/shard_map/psum | solution.py:161
  289.4 1.4 fusion.17
  290.8 10.4 %all_to_all.29 = f32[8,8,256]{2,1,0:T(8,128)S(1)} all-to-all(f32[8,8,256]{2,1,0:T(8,128)S(1)} %fusion.17), channel_id=1, replica_groups=mesh['req'=8,'head'=4] {'req'}, dimensions={0} | all-to-all | bytes 131072 | tf_op jit(solution)/shard_map/all_to_all | solution.py:212
  301.2 0.9 fusion.16
  302.1 0.7 fusion.70
  302.8 0.7 pad_maximum_fusion
  304.2 15.1 %reduce-scatter.2.cloned.1.call-done = f32[8,512]{1,0:T(8,128)} async-done(((f32[8,2048]{1,0:T(8,128)}), f32[8,512]{1,0:T(8,128)}) %reduce-scatter.2.cloned.1.call-update) | async-done | bytes 16400 | tf_op jit(solution)/shard_map/reduce_scatter | solution.py:213
  319.2 1.3 add_convert_fusion
  (77 shorter events, 6.9 us)
Async XLA Ops:
  7.2 102.9 %copy-start = (bf16[512,2048]{1,0:T(8,128)(2,1)S(1)}, bf16[512,2048]{1,0:T(8,128)(2,1)}, u32[]{:S(2)}) copy-start(bf16[512,2048]{1,0:T(8,128)(2,1)} %param.20) | copy-start | bytes 6291460
  7.2 9.8 %copy-start.11 = (f32[3,512]{1,0:T(4,128)S(1)}, f32[3,512]{1,0:T(4,128)}, u32[]{:S(2)}) copy-start(f32[3,512]{1,0:T(4,128)} %param.19) | copy-start | bytes 18436
  7.2 9.8 %copy-start.3 = (bf16[8,2048]{1,0:T(8,128)(2,1)S(1)}, bf16[8,2048]{1,0:T(8,128)(2,1)}, u32[]{:S(2)}) copy-start(bf16[8,2048]{1,0:T(8,128)(2,1)} %param.16) | copy-start | bytes 98308
  7.2 9.9 %copy-start.9 = (f32[2048]{0:T(1024)S(1)}, f32[2048]{0:T(1024)}, u32[]{:S(2)}) copy-start(f32[2048]{0:T(1024)} %param.17) | copy-start | bytes 24580
  7.2 138.7 %all-reduce.3.cloned.1.call-start = ((), (), s32[]{:S(2)}) async-start(), calls=%async_computation.4 | async-start | bytes 131072 | tf_op jit(solution)/shard_map/psum | solution.py:144
  21.6 0.6 copy-start.4
  66.6 8.1 %copy-start.16 = (bf16[8,2,4,512]{3,2,1,0:T(4,128)(2,1)S(1)}, bf16[8,2,4,512]{3,2,1,0:T(4,128)(2,1)}, u32[]{:S(2)}) copy-start(bf16[8,2,4,512]{3,2,1,0:T(4,128)(2,1)} %param.22) | copy-start | bytes 196612
  100.8 11.7 %copy-start.13 = (f32[8,4]{0,1:T(4,128)S(1)}, f32[8,4]{0,1:T(4,128)}, u32[]{:S(2)}) copy-start(f32[8,4]{0,1:T(4,128)} %param.25) | copy-start | bytes 388
  100.8 11.7 %copy-start.14 = (s32[8,4]{0,1:T(4,128)S(1)}, s32[8,4]{0,1:T(4,128)}, u32[]{:S(2)}) copy-start(s32[8,4]{0,1:T(4,128)} %param.24) | copy-start | bytes 388
  110.1 103.6 %copy-start.1 = (bf16[2,256,1408]{2,1,0:T(8,128)(2,1)S(1)}, bf16[2,256,1408]{2,1,0:T(8,128)(2,1)}, u32[]{:S(2)}) copy-start(bf16[2,256,1408]{2,1,0:T(8,128)(2,1)} %param.29) | copy-start | bytes 4325380
  121.2 84.5 %copy-start.8 = (f32[2048]{0:T(1024)S(1)}, f32[2048]{0:T(1024)}, u32[]{:S(2)}) copy-start(f32[2048]{0:T(1024)} %param.26) | copy-start | bytes 24580
  146.9 0.6 copy-start.2
  146.9 2.0 copy-start.12
  148.9 6.9 %collective-permute-start = (bf16[8,2048]{1,0:T(8,128)(2,1)}, bf16[8,2048]{1,0:T(8,128)(2,1)}, u32[]{:S(2)}, u32[]{:S(2)}) collective-permute-start(bf16[8,2048]{1,0:T(8,128)(2,1)} %multiply_convert_fusion), channel_id=1, source_target_pairs={{0,4},{4,8},{8,12},{12,16},{16,20},{20,24},{24,28},{28,0},{1,5},{5... | collective-permute-start | bytes 98312 | tf_op jit(solution)/shard_map/ppermute | solution.py:150
  155.9 6.9 %collective-permute-start.1 = (bf16[8,2048]{1,0:T(8,128)(2,1)}, bf16[8,2048]{1,0:T(8,128)(2,1)}, u32[]{:S(2)}, u32[]{:S(2)}) collective-permute-start(bf16[8,2048]{1,0:T(8,128)(2,1)} %collective-permute-done), channel_id=1, source_target_pairs={{0,4},{4,8},{8,12},{12,16},{16,20},{20,24},{24,28},{28,0},{1,5},{5... | collective-permute-start | bytes 98312 | tf_op jit(solution)/shard_map/ppermute | solution.py:150
  162.8 9.1 %collective-permute-start.2 = (bf16[8,2048]{1,0:T(8,128)(2,1)}, bf16[8,2048]{1,0:T(8,128)(2,1)}, u32[]{:S(2)}, u32[]{:S(2)}) collective-permute-start(bf16[8,2048]{1,0:T(8,128)(2,1)} %collective-permute-done.1), channel_id=1, source_target_pairs={{0,4},{4,8},{8,12},{12,16},{16,20},{20,24},{24,28},{28,0},{1,5},{5... | collective-permute-start | bytes 98312 | tf_op jit(solution)/shard_map/ppermute | solution.py:150
  165.8 27.6 %all-to-all-start = ((bf16[8,2,2048]{2,1,0:T(2,128)(2,1)}), bf16[8,2,2048]{2,1,0:T(2,128)(2,1)}, u32[]{:S(2)}, u32[]{:S(2)}) async-start(bf16[8,2,2048]{2,1,0:T(2,128)(2,1)} %reshape.198), calls=%async_computation | async-start | bytes 131072 | tf_op jit(solution)/shard_map/all_to_all | solution.py:200
  171.8 117.6 %all-reduce.5.cloned.1.call-start = ((), (), s32[]{:S(2)}) async-start(), calls=%async_computation.5 | async-start | bytes 1441792 | tf_op jit(solution)/shard_map/psum | solution.py:161
  171.9 7.3 %collective-permute-start.3 = (bf16[8,2048]{1,0:T(8,128)(2,1)}, bf16[8,2048]{1,0:T(8,128)(2,1)S(1)}, u32[]{:S(2)}, u32[]{:S(2)}) collective-permute-start(bf16[8,2048]{1,0:T(8,128)(2,1)} %collective-permute-done.2), channel_id=1, source_target_pairs={{0,4},{4,8},{8,12},{12,16},{16,20},{20,24},{24,28},{28,0},{1,5},{5... | collective-permute-start | bytes 98312 | tf_op jit(solution)/shard_map/ppermute | solution.py:150
  179.2 0.6 copy-start.7
  179.8 6.7 %collective-permute-start.4 = (bf16[8,2048]{1,0:T(8,128)(2,1)S(1)}, bf16[8,2048]{1,0:T(8,128)(2,1)}, u32[]{:S(2)}, u32[]{:S(2)}) collective-permute-start(bf16[8,2048]{1,0:T(8,128)(2,1)S(1)} %collective-permute-done.3), channel_id=1, source_target_pairs={{0,4},{4,8},{8,12},{12,16},{16,20},{20,24},{24,28},{28,0},{1,5},{5... | collective-permute-start | bytes 98312 | tf_op jit(solution)/shard_map/ppermute | solution.py:150
  186.5 6.9 %collective-permute-start.5 = (bf16[8,2048]{1,0:T(8,128)(2,1)}, bf16[8,2048]{1,0:T(8,128)(2,1)}, u32[]{:S(2)}, u32[]{:S(2)}) collective-permute-start(bf16[8,2048]{1,0:T(8,128)(2,1)} %collective-permute-done.4), channel_id=1, source_target_pairs={{0,4},{4,8},{8,12},{12,16},{16,20},{20,24},{24,28},{28,0},{1,5},{5... | collective-permute-start | bytes 98312 | tf_op jit(solution)/shard_map/ppermute | solution.py:150
  193.4 6.9 %collective-permute-start.6 = (bf16[8,2048]{1,0:T(8,128)(2,1)}, bf16[8,2048]{1,0:T(8,128)(2,1)}, u32[]{:S(2)}, u32[]{:S(2)}) collective-permute-start(bf16[8,2048]{1,0:T(8,128)(2,1)} %collective-permute-done.5), channel_id=1, source_target_pairs={{0,4},{4,8},{8,12},{12,16},{16,20},{20,24},{24,28},{28,0},{1,5},{5... | collective-permute-start | bytes 98312 | tf_op jit(solution)/shard_map/ppermute | solution.py:150
  212.8 0.8 copy-start.5
  213.6 13.3 %copy-start.10 = (f32[2048]{0:T(1024)S(1)}, f32[2048]{0:T(1024)}, u32[]{:S(2)}) copy-start(f32[2048]{0:T(1024)} %param.31) | copy-start | bytes 24580
  215.0 12.0 %copy-start.6 = (bf16[128,2048]{1,0:T(8,128)(2,1)S(1)}, bf16[128,2048]{1,0:T(8,128)(2,1)}, u32[]{:S(2)}) copy-start(bf16[128,2048]{1,0:T(8,128)(2,1)} %copy-done.5) | copy-start | bytes 1572868
  215.0 74.5 %copy-start.15 = (bf16[1408,256]{1,0:T(8,128)(2,1)S(1)}, bf16[1408,256]{1,0:T(8,128)(2,1)}, u32[]{:S(2)}) copy-start(bf16[1408,256]{1,0:T(8,128)(2,1)} %param.30) | copy-start | bytes 2162692
  223.0 67.7 %all-to-all-start.1 = ((f32[8,2,2048]{2,1,0:T(2,128)}), f32[8,2,2048]{2,1,0:T(2,128)S(1)}, u32[]{:S(2)}, u32[]{:S(2)}) async-start(f32[8,2,2048]{2,1,0:T(2,128)} %copy.50), calls=%async_computation.1 | async-start | bytes 262144 | tf_op jit(solution)/shard_map/all_to_all | solution.py:204
  226.9 92.3 %reduce-scatter.2.cloned.1.call-start = ((), (), s32[]{:S(2)}) async-start(), calls=%async_computation.6 | async-start | bytes 81920 | tf_op jit(solution)/shard_map/reduce_scatter | solution.py:213
Sparse Core Ops, SparseCore 0:
  112.1 33.8 all-reduce.2
  215.1 74.2 all-reduce.4
  302.2 16.9 reduce-scatter.1
